TPU v7x, 32 devices: a whole 2x2x4 slice. The times are simulated.
32 devices in a mesh: dp: 8 (over z, core), expert: 4 (over y, x).
Axes of the slice: x: 2, y: 2, z: 4, core: 2. Of those that a mesh axis runs over, the one named last changes fastest.
Arguments:
- embedded: bfloat16 [64, 197, 512], P(('dp', 'expert')), may hold values from -6 to 6
- cotangent: bfloat16 [64, 197, 512], P(('dp', 'expert')), may hold values from -6 to 6
- w_qkv: bfloat16 [2, 512, 1536], P(None, 'dp'), may hold values from -0.25 to 0.25
- w_proj: bfloat16 [2, 512, 512], P(None, 'dp'), may hold values from -2.5 to 2.5
- w_router: bfloat16 [2, 512, 8], P(None, 'dp'), may hold values from -0.1875 to 0.1875
- norm_gains: bfloat16 [2, 2, 512], P(None, None, 'dp'), may hold values from 0.25 to 1.75
- norm_shifts: bfloat16 [2, 2, 512], P(None, None, 'dp'), may hold values from -1 to 1
- w_first: bfloat16 [2, 8, 512, 2048], P(None, 'expert', None, 'dp'), may hold values from -0.25 to 0.25
- w_second: bfloat16 [2, 8, 2048, 512], P(None, 'expert', 'dp'), may hold values from -1 to 1
- routes: int32 [2, 64, 197, 2], P(None, ('dp', 'expert')), may hold values from 0 to 7, all different within a row; in each aligned block of 394 rows (0 to 393, 394 to 787, ..., all dimensions but the last counted through in order) at most 147 rows name the same one
Outputs:
- out_images: bfloat16 [64, 197, 512], P(('dp', 'expert'))
- grad_images: float32 [64, 197, 512], P(('dp', 'expert'))
- grad_qkv: float32 [2, 512, 1536], P(None, 'dp')
- grad_proj: float32 [2, 512, 512], P(None, 'dp')
- grad_router: float32 [2, 512, 8], P(None, 'dp')
- grad_gains: float32 [2, 2, 512], P(None, None, 'dp')
- grad_shifts: float32 [2, 2, 512], P(None, None, 'dp')
- grad_first: float32 [2, 8, 512, 2048], P(None, 'expert', None, 'dp')
- grad_second: float32 [2, 8, 2048, 512], P(None, 'expert', 'dp')
Inputs may be any that keep to these rules, and one draw needn't show every extreme that they name: `routes`: the two experts of a token differ. Among the 394 tokens of one device in one block, no expert is named by more than 147 tokens, a bound that some block reaches.
All inputs are finite; a program needn't handle non-finite values.
Results may differ from a plain program's by a relative error of at most 0.019.
Values may be sent and summed in bfloat16 or wider, within the bound.
No kernel may reach another device: no remote copies, remote signals or barrier semaphores. Data moves between devices by JAX's collectives and lax.ppermute only.
A program may use at most 192 MiB of HBM per device.

v0:
```python
import jax
import jax.numpy as jnp
from jax import lax
from jax.sharding import PartitionSpec as P

HEADS = 8
HEAD_DIM = 64
SEQ = 197
LAYERS = 2
EPSILON = 1e-06
ROOT_HALF = 0.7071067811865476
INV_ROOT_TAU = 0.3989422804014327


def layer_norm(values, scale_in, shift_in):
    center = values - jnp.mean(values, axis=-1, keepdims=True)
    variance = jnp.mean(center * center, axis=-1, keepdims=True)
    inverse = lax.rsqrt(variance + EPSILON)
    normed = center * inverse
    return (normed * scale_in + shift_in, normed, inverse)


def norm_back(grad_out, normed, inverse, scale_in):
    grad_normed = grad_out * scale_in
    first_mean = jnp.mean(grad_normed, axis=-1, keepdims=True)
    second_mean = jnp.mean(grad_normed * normed, axis=-1, keepdims=True)
    grad_in = inverse * (grad_normed - first_mean - normed * second_mean)
    return (grad_in, jnp.sum(grad_out * normed, axis=0), jnp.sum(grad_out, axis=0))


def softmax_rows(scores):
    highest = jnp.max(scores, axis=-1, keepdims=True)
    powers = jnp.exp(scores - highest)
    row_total = jnp.sum(powers, axis=-1, keepdims=True)
    return (powers / row_total, highest + jnp.log(row_total))


def gelu_value(preact):
    return 0.5 * preact * (1.0 + lax.erf(preact * ROOT_HALF))


def gelu_slope(preact):
    return (
        0.5 * (1.0 + lax.erf(preact * ROOT_HALF))
        + preact * jnp.exp(-0.5 * preact * preact) * INV_ROOT_TAU
    )


def layer_forward(
    resid, which, w_qkv, w_proj, w_router, norm_gains, norm_shifts, w_first, w_second, routes
):
    qkv_full, proj_full, router_full, gains_full, shifts_full = (
        lax.all_gather(w_qkv[which], "dp", axis=0, tiled=True),
        lax.all_gather(w_proj[which], "dp", axis=0, tiled=True),
        lax.all_gather(w_router[which], "dp", axis=0, tiled=True),
        lax.all_gather(norm_gains[which], "dp", axis=1, tiled=True),
        lax.all_gather(norm_shifts[which], "dp", axis=1, tiled=True),
    )
    first_full, second_full = (
        lax.all_gather(w_first[which], "dp", axis=2, tiled=True),
        lax.all_gather(w_second[which], "dp", axis=1, tiled=True),
    )
    tok_count, width = resid.shape
    images = tok_count // SEQ
    gains_wide = gains_full.astype(jnp.float32)
    shifts_wide = shifts_full.astype(jnp.float32)
    attn_norm, unit_a, inv_a = layer_norm(resid, gains_wide[0], shifts_wide[0])
    attn_in = attn_norm.astype(jnp.bfloat16)
    packed = jnp.dot(attn_in, qkv_full, preferred_element_type=jnp.float32)
    head_shape = (images, SEQ, HEADS, HEAD_DIM)
    query = (packed[:, :width] * HEAD_DIM ** (-0.5)).astype(jnp.bfloat16).reshape(head_shape)
    keyed = packed[:, width : 2 * width].astype(jnp.bfloat16).reshape(head_shape)
    valued = packed[:, 2 * width :].astype(jnp.bfloat16).reshape(head_shape)
    scores = jnp.einsum("iqhd,ikhd->ihqk", query, keyed, preferred_element_type=jnp.float32)
    probs, log_total = softmax_rows(scores)
    mixed = jnp.einsum(
        "ihqk,ikhd->iqhd", probs.astype(jnp.bfloat16), valued, preferred_element_type=jnp.float32
    )
    mixed = mixed.reshape(tok_count, width).astype(jnp.bfloat16)
    resid_mid = resid + jnp.dot(mixed, proj_full, preferred_element_type=jnp.float32)
    moe_norm, unit_b, inv_b = layer_norm(resid_mid, gains_wide[1], shifts_wide[1])
    moe_in = moe_norm.astype(jnp.bfloat16)
    logits = jnp.dot(moe_in, router_full, preferred_element_type=jnp.float32)
    router_probs, ignored_total = softmax_rows(logits)
    experts_total = router_full.shape[1]
    local_count = first_full.shape[0]
    peers = lax.axis_size("expert")
    capacity = max(2, 3 * tok_count // experts_total)
    route = routes[which].reshape(tok_count, 2)
    labels = jnp.arange(experts_total, dtype=jnp.int32)
    pick_first = (route[:, 0:1] == labels[None, :]).astype(jnp.int32)
    pick_second = (route[:, 1:2] == labels[None, :]).astype(jnp.int32)
    both_picks = pick_first + pick_second
    before = jnp.cumsum(both_picks, axis=0) - both_picks
    slot_first = route[:, 0] * capacity + jnp.sum(before * pick_first, axis=1)
    slot_second = route[:, 1] * capacity + jnp.sum(before * pick_second, axis=1)
    slot_ids = jnp.arange(experts_total * capacity, dtype=jnp.int32)
    place_first = (slot_ids[:, None] == slot_first[None, :]).astype(jnp.bfloat16)
    place_second = (slot_ids[:, None] == slot_second[None, :]).astype(jnp.bfloat16)
    outgoing = jnp.dot(place_first + place_second, moe_in, preferred_element_type=jnp.float32)
    outgoing = outgoing.astype(jnp.bfloat16).reshape(peers, local_count, capacity, width)
    incoming = lax.all_to_all(outgoing, "expert", split_axis=0, concat_axis=0, tiled=True)
    hidden_pre = jnp.einsum(
        "sjcd,jdf->sjcf", incoming, first_full, preferred_element_type=jnp.float32
    )
    hidden_act = gelu_value(hidden_pre).astype(jnp.bfloat16)
    result = jnp.einsum(
        "sjcf,jfd->sjcd", hidden_act, second_full, preferred_element_type=jnp.float32
    ).astype(jnp.bfloat16)
    returned = lax.all_to_all(result, "expert", split_axis=0, concat_axis=0, tiled=True).reshape(
        experts_total * capacity, width
    )
    pick_first_f = pick_first.astype(jnp.float32)
    pick_second_f = pick_second.astype(jnp.float32)
    gate_first = jnp.sum(router_probs * pick_first_f, axis=1)
    gate_second = jnp.sum(router_probs * pick_second_f, axis=1)
    back_first = jnp.take(returned, slot_first, axis=0).astype(jnp.float32)
    back_second = jnp.take(returned, slot_second, axis=0).astype(jnp.float32)
    resid_out = resid_mid + (gate_first[:, None] * back_first + gate_second[:, None] * back_second)
    saved = (
        qkv_full,
        proj_full,
        router_full,
        gains_wide,
        first_full,
        second_full,
        unit_a,
        inv_a,
        attn_in,
        query,
        keyed,
        valued,
        log_total,
        mixed,
        unit_b,
        inv_b,
        moe_in,
        router_probs,
        pick_first_f,
        pick_second_f,
        slot_first,
        slot_second,
        place_first,
        place_second,
        incoming,
        hidden_pre,
        hidden_act,
        returned,
        gate_first,
        gate_second,
    )
    return (resid_out, saved)


def layer_backward(grad_out, saved):
    (
        qkv_full,
        proj_full,
        router_full,
        gains_wide,
        first_full,
        second_full,
        unit_a,
        inv_a,
        attn_in,
        query,
        keyed,
        valued,
        log_total,
        mixed,
        unit_b,
        inv_b,
        moe_in,
        router_probs,
        pick_first_f,
        pick_second_f,
        slot_first,
        slot_second,
        place_first,
        place_second,
        incoming,
        hidden_pre,
        hidden_act,
        returned,
        gate_first,
        gate_second,
    ) = saved
    tok_count, width = grad_out.shape
    images = tok_count // SEQ
    back_first = jnp.take(returned, slot_first, axis=0).astype(jnp.float32)
    back_second = jnp.take(returned, slot_second, axis=0).astype(jnp.float32)
    grad_gate_first = jnp.sum(grad_out * back_first, axis=1)
    grad_gate_second = jnp.sum(grad_out * back_second, axis=1)
    send_first = (gate_first[:, None] * grad_out).astype(jnp.bfloat16)
    send_second = (gate_second[:, None] * grad_out).astype(jnp.bfloat16)
    slot_grads = jnp.dot(place_first, send_first, preferred_element_type=jnp.float32) + jnp.dot(
        place_second, send_second, preferred_element_type=jnp.float32
    )
    slot_grads = slot_grads.astype(jnp.bfloat16).reshape(incoming.shape)
    grad_result = lax.all_to_all(slot_grads, "expert", split_axis=0, concat_axis=0, tiled=True)
    grad_act = jnp.einsum(
        "sjcd,jfd->sjcf", grad_result, second_full, preferred_element_type=jnp.float32
    )
    grad_second = jnp.einsum(
        "sjcf,sjcd->jfd", hidden_act, grad_result, preferred_element_type=jnp.float32
    )
    grad_pre = (grad_act * gelu_slope(hidden_pre)).astype(jnp.bfloat16)
    grad_first = jnp.einsum(
        "sjcd,sjcf->jdf", incoming, grad_pre, preferred_element_type=jnp.float32
    )
    grad_rows = jnp.einsum(
        "sjcf,jdf->sjcd", grad_pre, first_full, preferred_element_type=jnp.float32
    ).astype(jnp.bfloat16)
    grad_back = lax.all_to_all(
        grad_rows, "expert", split_axis=0, concat_axis=0, tiled=True
    ).reshape(-1, width)
    grad_moe = jnp.einsum(
        "st,sd->td", place_first + place_second, grad_back, preferred_element_type=jnp.float32
    )
    grad_probs = pick_first_f * grad_gate_first[:, None] + pick_second_f * grad_gate_second[:, None]
    weighted = jnp.sum(router_probs * grad_probs, axis=1, keepdims=True)
    grad_logits = (router_probs * (grad_probs - weighted)).astype(jnp.bfloat16)
    grad_router = jnp.einsum("td,te->de", moe_in, grad_logits, preferred_element_type=jnp.float32)
    grad_moe = grad_moe + jnp.einsum(
        "te,de->td", grad_logits, router_full, preferred_element_type=jnp.float32
    )
    grad_norm_b, gain_b_grad, shift_b_grad = norm_back(grad_moe, unit_b, inv_b, gains_wide[1])
    grad_mid = grad_out + grad_norm_b
    grad_branch = grad_mid.astype(jnp.bfloat16)
    grad_proj = jnp.einsum("td,te->de", mixed, grad_branch, preferred_element_type=jnp.float32)
    grad_mixed = jnp.einsum("te,de->td", grad_branch, proj_full, preferred_element_type=jnp.float32)
    grad_mixed = grad_mixed.astype(jnp.bfloat16).reshape(images, SEQ, HEADS, HEAD_DIM)
    scores = jnp.einsum("iqhd,ikhd->ihqk", query, keyed, preferred_element_type=jnp.float32)
    probs = jnp.exp(scores - log_total)
    grad_weights = jnp.einsum(
        "iqhd,ikhd->ihqk", grad_mixed, valued, preferred_element_type=jnp.float32
    )
    grad_valued = jnp.einsum(
        "ihqk,iqhd->ikhd",
        probs.astype(jnp.bfloat16),
        grad_mixed,
        preferred_element_type=jnp.float32,
    ).astype(jnp.bfloat16)
    row_inner = jnp.sum(probs * grad_weights, axis=-1, keepdims=True)
    grad_scores = (probs * (grad_weights - row_inner)).astype(jnp.bfloat16)
    grad_query = jnp.einsum(
        "ihqk,ikhd->iqhd", grad_scores, keyed, preferred_element_type=jnp.float32
    ).astype(jnp.bfloat16)
    grad_query = grad_query * jnp.asarray(HEAD_DIM ** (-0.5), jnp.bfloat16)
    grad_keyed = jnp.einsum(
        "ihqk,iqhd->ikhd", grad_scores, query, preferred_element_type=jnp.float32
    ).astype(jnp.bfloat16)
    grad_packed = jnp.concatenate(
        [
            grad_query.reshape(tok_count, width),
            grad_keyed.reshape(tok_count, width),
            grad_valued.reshape(tok_count, width),
        ],
        axis=1,
    )
    grad_qkv = jnp.einsum("td,te->de", attn_in, grad_packed, preferred_element_type=jnp.float32)
    grad_attn = jnp.einsum("te,de->td", grad_packed, qkv_full, preferred_element_type=jnp.float32)
    grad_norm_a, gain_a_grad, shift_a_grad = norm_back(grad_attn, unit_a, inv_a, gains_wide[0])
    grad_in = grad_mid + grad_norm_a
    dense = (
        grad_qkv,
        grad_proj,
        grad_router,
        jnp.stack([gain_a_grad, gain_b_grad]),
        jnp.stack([shift_a_grad, shift_b_grad]),
    )
    return (grad_in, dense, (grad_first, grad_second))


def body(
    embedded, cotangent, w_qkv, w_proj, w_router, norm_gains, norm_shifts, w_first, w_second, routes
):
    images, length, width = embedded.shape
    tok_count = images * length
    resid = embedded.reshape(tok_count, width).astype(jnp.float32)
    layer_inputs = []
    for which in range(LAYERS):
        layer_inputs.append(resid)
        resid, saved = layer_forward(
            resid,
            which,
            w_qkv,
            w_proj,
            w_router,
            norm_gains,
            norm_shifts,
            w_first,
            w_second,
            routes,
        )
    out_images = resid.reshape(images, length, width).astype(jnp.bfloat16)
    grad = cotangent.reshape(tok_count, width).astype(jnp.float32)
    dense_layers = []
    expert_layers = []
    for which in reversed(range(LAYERS)):
        ignored, saved = layer_forward(
            layer_inputs[which],
            which,
            w_qkv,
            w_proj,
            w_router,
            norm_gains,
            norm_shifts,
            w_first,
            w_second,
            routes,
        )
        grad, dense, expert_part = layer_backward(grad, saved)
        totals = (
            lax.psum(dense[0].astype(jnp.bfloat16), "expert").astype(jnp.float32),
            lax.psum(dense[1].astype(jnp.bfloat16), "expert").astype(jnp.float32),
            lax.psum(dense[2].astype(jnp.bfloat16), "expert").astype(jnp.float32),
            lax.psum(dense[3].astype(jnp.bfloat16), "expert").astype(jnp.float32),
            lax.psum(dense[4].astype(jnp.bfloat16), "expert").astype(jnp.float32),
        )
        shares = (
            lax.psum_scatter(
                totals[0].astype(jnp.bfloat16), "dp", scatter_dimension=0, tiled=True
            ).astype(jnp.float32),
            lax.psum_scatter(
                totals[1].astype(jnp.bfloat16), "dp", scatter_dimension=0, tiled=True
            ).astype(jnp.float32),
            lax.psum_scatter(
                totals[2].astype(jnp.bfloat16), "dp", scatter_dimension=0, tiled=True
            ).astype(jnp.float32),
            lax.psum_scatter(
                totals[3].astype(jnp.bfloat16), "dp", scatter_dimension=1, tiled=True
            ).astype(jnp.float32),
            lax.psum_scatter(
                totals[4].astype(jnp.bfloat16), "dp", scatter_dimension=1, tiled=True
            ).astype(jnp.float32),
        )
        expert_shares = (
            lax.psum_scatter(
                expert_part[0].astype(jnp.bfloat16), "dp", scatter_dimension=2, tiled=True
            ).astype(jnp.float32),
            lax.psum_scatter(
                expert_part[1].astype(jnp.bfloat16), "dp", scatter_dimension=1, tiled=True
            ).astype(jnp.float32),
        )
        dense_layers.insert(0, shares)
        expert_layers.insert(0, expert_shares)
    grad_images = grad.reshape(images, length, width)
    grad_qkv = jnp.stack([entry[0] for entry in dense_layers])
    grad_proj = jnp.stack([entry[1] for entry in dense_layers])
    grad_router = jnp.stack([entry[2] for entry in dense_layers])
    grad_gains = jnp.stack([entry[3] for entry in dense_layers])
    grad_shifts = jnp.stack([entry[4] for entry in dense_layers])
    grad_first = jnp.stack([entry[0] for entry in expert_layers])
    grad_second = jnp.stack([entry[1] for entry in expert_layers])
    return (
        out_images,
        grad_images,
        grad_qkv,
        grad_proj,
        grad_router,
        grad_gains,
        grad_shifts,
        grad_first,
        grad_second,
    )


def solution(mesh):
    return jax.shard_map(
        body,
        mesh=mesh,
        in_specs=(
            P(("dp", "expert"), None, None),
            P(("dp", "expert"), None, None),
            P(None, "dp", None),
            P(None, "dp", None),
            P(None, "dp", None),
            P(None, None, "dp"),
            P(None, None, "dp"),
            P(None, "expert", None, "dp"),
            P(None, "expert", "dp", None),
            P(None, ("dp", "expert"), None, None),
        ),
        out_specs=(
            P(("dp", "expert"), None, None),
            P(("dp", "expert"), None, None),
            P(None, "dp", None),
            P(None, "dp", None),
            P(None, "dp", None),
            P(None, None, "dp"),
            P(None, None, "dp"),
            P(None, "expert", None, "dp"),
            P(None, "expert", "dp", None),
        ),
        check_vma=False,
    )
```

profile of v0, /device:TPU:0, one launch (start us, length us, event | category | flops | bytes accessed | tf_op | source)
XLA Modules:
  0.0 1092.9 jit_solution(856967177096205174)
XLA Ops:
  16.5 17.0 %all-gather = bf16[1,2,512]{1,0,2:T(2,128)(2,1)S(1)} all-gather(bf16[1,2,64]{1,0,2:T(2,128)(2,1)S(1)} %copy.377), channel_id=2, replica_groups=mesh['dp'=8,'expert'=4] {'dp'}, dimensions={2}, use_global_device_ids=true | all-gather | bytes 2304 | tf_op jit(solution)/shard_map/all_gather | solution.py:56
  37.7 14.6 %all-gather.1 = bf16[1,2,512]{1,0,2:T(2,128)(2,1)S(1)} all-gather(bf16[1,2,64]{1,0,2:T(2,128)(2,1)S(1)} %copy.378), channel_id=3, replica_groups=mesh['dp'=8,'expert'=4] {'dp'}, dimensions={2}, use_global_device_ids=true | all-gather | bytes 2304 | tf_op jit(solution)/shard_map/all_gather | solution.py:57
  55.9 25.2 %all-gather.3 = bf16[1,512,512]{2,1,0:T(8,128)(2,1)} all-gather(bf16[1,64,512]{2,1,0:T(8,128)(2,1)S(1)} %get-tuple-element.126), channel_id=5, replica_groups=mesh['dp'=8,'expert'=4] {'dp'}, dimensions={1}, use_global_device_ids=true | all-gather | bytes 589824 | tf_op jit(solution)/shard_map/all_gather | solution.py:54
  122.9 15.7 %all-gather.4 = bf16[1,512,8]{2,0,1:T(2,128)(2,1)S(1)} all-gather(bf16[1,64,8]{2,0,1:T(2,128)(2,1)} %copy.379), channel_id=6, replica_groups=mesh['dp'=8,'expert'=4] {'dp'}, dimensions={1}, use_global_device_ids=true | all-gather | bytes 9216 | tf_op jit(solution)/shard_map/all_gather | solution.py:55
  140.0 14.2 %all-gather.7 = bf16[1,2,512]{1,0,2:T(2,128)(2,1)S(1)} all-gather(bf16[1,2,64]{1,0,2:T(2,128)(2,1)S(1)} %copy.380), channel_id=9, replica_groups=mesh['dp'=8,'expert'=4] {'dp'}, dimensions={2}, use_global_device_ids=true | all-gather | bytes 2304 | tf_op jit(solution)/shard_map/all_gather | solution.py:56
  155.8 15.6 %all-gather.8 = bf16[1,2,512]{1,0,2:T(2,128)(2,1)S(1)} all-gather(bf16[1,2,64]{1,0,2:T(2,128)(2,1)} %copy.381), channel_id=10, replica_groups=mesh['dp'=8,'expert'=4] {'dp'}, dimensions={2}, use_global_device_ids=true | all-gather | bytes 2304 | tf_op jit(solution)/shard_map/all_gather | solution.py:57
  206.3 17.5 %all-gather.10 = bf16[1,512,512]{2,1,0:T(8,128)(2,1)} all-gather(bf16[1,64,512]{2,1,0:T(8,128)(2,1)S(1)} %copy-done.50), channel_id=12, replica_groups=mesh['dp'=8,'expert'=4] {'dp'}, dimensions={1}, use_global_device_ids=true | all-gather | bytes 589824 | tf_op jit(solution)/shard_map/all_gather | solution.py:54
  287.3 14.8 %all-gather.11 = bf16[1,512,8]{2,0,1:T(2,128)(2,1)S(1)} all-gather(bf16[1,64,8]{2,0,1:T(2,128)(2,1)} %copy.382), channel_id=13, replica_groups=mesh['dp'=8,'expert'=4] {'dp'}, dimensions={1}, use_global_device_ids=true | all-gather | bytes 9216 | tf_op jit(solution)/shard_map/all_gather | solution.py:55
  330.4 15.1 %all-to-all-done.3 = bf16[4,2,147,512]{3,1,2,0:T(2,128)(2,1)} async-done(((bf16[4,2,147,512]{3,1,2,0:T(2,128)(2,1)}), bf16[4,2,147,512]{3,1,2,0:T(2,128)(2,1)}, u32[]{:S(2)}, u32[]{:S(2)}) %all-to-all-start.3) | async-done | bytes 1204256 | tf_op jit(solution)/shard_map/all_to_all | solution.py:110
  369.8 18.9 %all_to_all.44 = bf16[4,2,147,512]{3,1,2,0:T(2,128)(2,1)S(1)} all-to-all(bf16[4,2,147,512]{3,1,2,0:T(2,128)(2,1)S(1)} %copy.295), channel_id=1, replica_groups=mesh['dp'=8,'expert'=4] {'expert'}, dimensions={0} | all-to-all | bytes 2408448 | tf_op jit(solution)/shard_map/all_to_all | solution.py:200
  406.2 14.4 %all-to-all-done.5 = bf16[4,2,147,512]{3,1,2,0:T(2,128)(2,1)} async-done(((bf16[4,2,147,512]{3,1,2,0:T(2,128)(2,1)}), bf16[4,2,147,512]{3,1,2,0:T(2,128)(2,1)}, u32[]{:S(2)}, u32[]{:S(2)}) %all-to-all-start.5) | async-done | bytes 1204256 | tf_op jit(solution)/shard_map/all_to_all | solution.py:214
  471.1 18.4 %all_to_all.45 = bf16[4,2,147,512]{3,1,2,0:T(2,128)(2,1)S(1)} all-to-all(bf16[4,2,147,512]{3,1,2,0:T(2,128)(2,1)S(1)} %copy.311), channel_id=1, replica_groups=mesh['dp'=8,'expert'=4] {'expert'}, dimensions={0} | all-to-all | bytes 2408448 | tf_op jit(solution)/shard_map/all_to_all | solution.py:200
  574.3 35.1 %reduce-scatter.37.cloned.1.call-done = bf16[64,1536]{1,0:T(8,128)(2,1)} async-done(((bf16[512,1536]{1,0:T(8,128)(2,1)}), bf16[64,1536]{1,0:T(8,128)(2,1)}) %reduce-scatter.37.cloned.1.call-update) | async-done | bytes 196624 | tf_op jit(solution)/shard_map/reduce_scatter | solution.py:322
  609.4 34.7 %reduce-scatter.35.cloned.1.call-done = bf16[64,1536]{1,0:T(8,128)(2,1)} async-done(((bf16[512,1536]{1,0:T(8,128)(2,1)}), bf16[64,1536]{1,0:T(8,128)(2,1)}) %reduce-scatter.35.cloned.1.call-update) | async-done | bytes 196624 | tf_op jit(solution)/shard_map/reduce_scatter | solution.py:322
  681.8 25.0 %reduce-scatter.53.cloned.1.call-done = bf16[64,2]{1,0:T(8,128)(2,1)} async-done(((bf16[512,2]{1,0:T(8,128)(2,1)}), bf16[64,2]{1,0:T(8,128)(2,1)}) %reduce-scatter.53.cloned.1.call-update) | async-done | bytes 272
  707.6 30.8 %reduce-scatter.49.cloned.1.call-done = bf16[64,2]{1,0:T(8,128)(2,1)} async-done(((bf16[512,2]{1,0:T(8,128)(2,1)}), bf16[64,2]{1,0:T(8,128)(2,1)}) %reduce-scatter.49.cloned.1.call-update) | async-done | bytes 272
  739.2 30.7 %reduce-scatter.43.cloned.1.call-done = bf16[64,8]{1,0:T(8,128)(2,1)} async-done(((bf16[512,8]{1,0:T(8,128)(2,1)}), bf16[64,8]{1,0:T(8,128)(2,1)}) %reduce-scatter.43.cloned.1.call-update) | async-done | bytes 1040
  772.6 28.1 %reduce-scatter.51.cloned.1.call-done = bf16[64,2]{1,0:T(8,128)(2,1)} async-done(((bf16[512,2]{1,0:T(8,128)(2,1)}), bf16[64,2]{1,0:T(8,128)(2,1)}) %reduce-scatter.51.cloned.1.call-update) | async-done | bytes 272
  801.5 30.6 %reduce-scatter.47.cloned.1.call-done = bf16[64,2]{1,0:T(8,128)(2,1)} async-done(((bf16[512,2]{1,0:T(8,128)(2,1)}), bf16[64,2]{1,0:T(8,128)(2,1)}) %reduce-scatter.47.cloned.1.call-update) | async-done | bytes 272
  844.7 34.3 %all-reduce.6.cloned.1.call-done = (bf16[64,1536]{1,0:T(8,128)(2,1)}, bf16[64,1536]{1,0:T(8,128)(2,1)}, bf16[64,512]{1,0:T(8,128)(2,1)}, bf16[64,512]{1,0:T(8,128)(2,1)}) async-done(((bf16[64,1536]{1,0:T(8,128)(2,1)}, bf16[64,1536]{1,0:T(8,128)(2,1)}, bf16[64,512]{1,0:T(8,128)(2,1)}, bf16[64,512]{1,0:T(8,128)(2,1)}), (bf16[64,1536]{1,0:T(8,128)(2,1)}, bf16[64,1536]{1,0:T(8,128)(2,1)}, ...) | async-done | bytes 524304 | tf_op jit(solution)/shard_map/psum | solution.py:315
  882.6 48.5 %reduce-scatter.33.cloned.1.call-done = bf16[2,256,512]{2,1,0:T(8,128)(2,1)} async-done(((bf16[2,2048,512]{2,1,0:T(8,128)(2,1)}), bf16[2,256,512]{2,1,0:T(8,128)(2,1)}) %reduce-scatter.33.cloned.1.call-update) | async-done | bytes 524304 | tf_op jit(solution)/shard_map/reduce_scatter | solution.py:342
  931.1 50.7 %reduce-scatter.31.cloned.1.call-done = bf16[2,256,512]{2,1,0:T(8,128)(2,1)} async-done(((bf16[2,2048,512]{2,1,0:T(8,128)(2,1)}), bf16[2,256,512]{2,1,0:T(8,128)(2,1)}) %reduce-scatter.31.cloned.1.call-update) | async-done | bytes 524304 | tf_op jit(solution)/shard_map/reduce_scatter | solution.py:342
  984.5 47.9 %reduce-scatter.29.cloned.1.call-done = bf16[2,512,256]{2,1,0:T(8,128)(2,1)} async-done(((bf16[2,512,2048]{2,1,0:T(8,128)(2,1)}), bf16[2,512,256]{2,1,0:T(8,128)(2,1)}) %reduce-scatter.29.cloned.1.call-update) | async-done | bytes 524304 | tf_op jit(solution)/shard_map/reduce_scatter | solution.py:339
  1032.4 50.7 %reduce-scatter.27.cloned.1.call-done = bf16[2,512,256]{2,1,0:T(8,128)(2,1)} async-done(((bf16[2,512,2048]{2,1,0:T(8,128)(2,1)}), bf16[2,512,256]{2,1,0:T(8,128)(2,1)}) %reduce-scatter.27.cloned.1.call-update) | async-done | bytes 524304 | tf_op jit(solution)/shard_map/reduce_scatter | solution.py:339
  (595 shorter events, 427.7 us)
Async XLA Ops:
  7.2 80.8 %all-gather.21.cloned.1.call-start = ((), (), s32[]{:S(2)}) async-start(), calls=%async_computation.26 | async-start | bytes 1769472 | tf_op jit(solution)/shard_map/all_gather | solution.py:53
  9.1 174.3 %all-gather.23.cloned.1.call-start = ((), (), s32[]{:S(2)}) async-start(), calls=%async_computation.27 | async-start | bytes 4718592 | tf_op jit(solution)/shard_map/all_gather | solution.py:60
  11.5 181.1 %all-gather.25.cloned.1.call-start = ((), (), s32[]{:S(2)}) async-start(), calls=%async_computation.28 | async-start | bytes 4718592 | tf_op jit(solution)/shard_map/all_gather | solution.py:61
  12.6 229.4 %all-gather.27.cloned.1.call-start = ((), (), s32[]{:S(2)}) async-start(), calls=%async_computation.29 | async-start | bytes 1769472 | tf_op jit(solution)/shard_map/all_gather | solution.py:53
  13.2 293.7 %all-gather.29.cloned.1.call-start = ((), (), s32[]{:S(2)}) async-start(), calls=%async_computation.30 | async-start | bytes 4718592 | tf_op jit(solution)/shard_map/all_gather | solution.py:60
  13.8 302.3 %all-gather.31.cloned.1.call-start = ((), (), s32[]{:S(2)}) async-start(), calls=%async_computation.31 | async-start | bytes 4718592 | tf_op jit(solution)/shard_map/all_gather | solution.py:61
  118.6 64.8 %all-to-all-start = ((bf16[4,2,147,512]{3,1,2,0:T(2,128)(2,1)}), bf16[4,2,147,512]{3,1,2,0:T(2,128)(2,1)}, u32[]{:S(2)}, u32[]{:S(2)}) async-start(bf16[4,2,147,512]{3,1,2,0:T(2,128)(2,1)} %copy.273), calls=%async_computation | async-start | bytes 2408448 | tf_op jit(solution)/shard_map/all_to_all | solution.py:102
  201.4 23.8 %all-to-all-start.1 = ((bf16[4,2,147,512]{3,1,2,0:T(2,128)(2,1)}), bf16[4,2,147,512]{3,1,2,0:T(2,128)(2,1)}, u32[]{:S(2)}, u32[]{:S(2)}) async-start(bf16[4,2,147,512]{3,1,2,0:T(2,128)(2,1)} %copy.275), calls=%async_computation.1 | async-start | bytes 2408448 | tf_op jit(solution)/shard_map/all_to_all | solution.py:110
  282.2 24.7 %all-to-all-start.2 = ((bf16[4,2,147,512]{3,1,2,0:T(2,128)(2,1)}), bf16[4,2,147,512]{3,1,2,0:T(2,128)(2,1)}, u32[]{:S(2)}, u32[]{:S(2)}) async-start(bf16[4,2,147,512]{3,1,2,0:T(2,128)(2,1)} %copy.290), calls=%async_computation.2 | async-start | bytes 2408448 | tf_op jit(solution)/shard_map/all_to_all | solution.py:102
  507.1 62.2 %reduce-scatter.41.cloned.1.call-start = ((), (), s32[]{:S(2)}) async-start(), calls=%async_computation.35 | async-start | bytes 589824 | tf_op jit(solution)/shard_map/reduce_scatter | solution.py:325
  509.7 64.6 %reduce-scatter.39.cloned.1.call-start = ((), (), s32[]{:S(2)}) async-start(), calls=%async_computation.34 | async-start | bytes 589824 | tf_op jit(solution)/shard_map/reduce_scatter | solution.py:325
  532.0 77.4 %reduce-scatter.37.cloned.1.call-start = ((), (), s32[]{:S(2)}) async-start(), calls=%async_computation.33 | async-start | bytes 1769472 | tf_op jit(solution)/shard_map/reduce_scatter | solution.py:322
  536.1 108.0 %reduce-scatter.35.cloned.1.call-start = ((), (), s32[]{:S(2)}) async-start(), calls=%async_computation.32 | async-start | bytes 1769472 | tf_op jit(solution)/shard_map/reduce_scatter | solution.py:322
  560.0 119.7 %reduce-scatter.45.cloned.1.call-start = ((), (), s32[]{:S(2)}) async-start(), calls=%async_computation.37 | async-start | bytes 147456
  561.0 145.8 %reduce-scatter.53.cloned.1.call-start = ((), (), s32[]{:S(2)}) async-start(), calls=%async_computation.41 | async-start | bytes 147456
  561.9 176.5 %reduce-scatter.49.cloned.1.call-start = ((), (), s32[]{:S(2)}) async-start(), calls=%async_computation.39 | async-start | bytes 147456
  562.9 207.0 %reduce-scatter.43.cloned.1.call-start = ((), (), s32[]{:S(2)}) async-start(), calls=%async_computation.36 | async-start | bytes 147456
  563.9 236.8 %reduce-scatter.51.cloned.1.call-start = ((), (), s32[]{:S(2)}) async-start(), calls=%async_computation.40 | async-start | bytes 147456
  568.2 263.8 %reduce-scatter.47.cloned.1.call-start = ((), (), s32[]{:S(2)}) async-start(), calls=%async_computation.38 | async-start | bytes 147456
  569.1 309.9 %all-reduce.6.cloned.1.call-start = ((), (), s32[]{:S(2)}) async-start(), calls=%async_computation.42 | async-start | bytes 1048576 | tf_op jit(solution)/shard_map/psum | solution.py:315
  644.1 287.0 %reduce-scatter.33.cloned.1.call-start = ((), (), s32[]{:S(2)}) async-start(), calls=%async_computation.25 | async-start | bytes 4718592 | tf_op jit(solution)/shard_map/reduce_scatter | solution.py:342
  652.8 329.1 %reduce-scatter.31.cloned.1.call-start = ((), (), s32[]{:S(2)}) async-start(), calls=%async_computation.24 | async-start | bytes 4718592 | tf_op jit(solution)/shard_map/reduce_scatter | solution.py:342
  662.6 369.8 %reduce-scatter.29.cloned.1.call-start = ((), (), s32[]{:S(2)}) async-start(), calls=%async_computation.23 | async-start | bytes 4718592 | tf_op jit(solution)/shard_map/reduce_scatter | solution.py:339
  671.0 412.1 %reduce-scatter.27.cloned.1.call-start = ((), (), s32[]{:S(2)}) async-start(), calls=%async_computation.22 | async-start | bytes 4718592 | tf_op jit(solution)/shard_map/reduce_scatter | solution.py:339
  (142 other events, 1518.4 us)
Sparse Core Ops, SparseCore 0:
  10.2 29.4 all-gather.20
  41.3 51.4 all-gather.22
  94.4 47.3 all-gather.24
  143.9 25.8 all-gather.26
  171.2 49.7 all-gather.28
  222.4 45.8 all-gather.30
  510.1 32.3 reduce-scatter.40
  544.8 29.4 reduce-scatter.38
  577.2 32.1 reduce-scatter.36
  611.6 32.4 reduce-scatter.34
  646.9 28.9 reduce-scatter.44
  678.1 28.7 reduce-scatter.52
  709.6 28.7 reduce-scatter.48
  741.1 28.7 reduce-scatter.42
  771.9 28.7 reduce-scatter.50
  803.4 28.6 reduce-scatter.46
  835.2 43.8 all-reduce.5
  881.2 49.8 reduce-scatter.32
  933.4 48.3 reduce-scatter.30
  984.0 48.3 reduce-scatter.28
  1034.7 48.3 reduce-scatter.26
where the time goes:
time: 1100 us; the launch traced here: 1090 us
  waiting for transfers between devices  495 us (45%)
  local copies, waits for them, and re-layouts  186 us (17%)
  blocking collectives  182 us (17%)
  matrix products  151 us (14%)
  other arithmetic  35 us (3%)
  starting transfers between devices  27.2 us (2%)
  between operations  16.6 us (2%)
    unnamed x27, waiting for transfers between devices  147 us
    reduce_scatter x2, waiting for transfers between devices, body(): lax.psum_scatter(expert_part[1].astype(jnp.bfloat16), 'dp', scatter_dimen...  99.3 us
    reduce_scatter x2, waiting for transfers between devices, body(): lax.psum_scatter(expert_part[0].astype(jnp.bfloat16), 'dp', scatter_dimen...  98.6 us
    reduce_scatter x2, waiting for transfers between devices, body(): lax.psum_scatter(totals[0].astype(jnp.bfloat16), 'dp', scatter_dimension=...  69.8 us
    all_gather x2, blocking collectives, layer_forward(): lax.all_gather(w_proj[which], 'dp', axis=0, tiled=True)  42.8 us
    all_to_all x2, blocking collectives, layer_backward(): lax.all_to_all(slot_grads, 'expert', split_axis=0, concat_axis=0, tiled=T...  37.3 us
    psum x1, waiting for transfers between devices, body(): lax.psum(dense[0].astype(jnp.bfloat16), 'expert').astype(jnp.float32)  34.3 us
    unnamed x304, local copies, waits for them, and re-layouts  32.4 us
  transfers between devices with their start and end apart: 27, of which 16 were waited for; matrix products, arithmetic and copies ran while one was open for 23% of the time, Pallas kernels for 0%

commit v1 on v0

--- a/solution.py
+++ b/solution.py
@@ -10,6 +10,11 @@
 EPSILON = 1e-06
 ROOT_HALF = 0.7071067811865476
 INV_ROOT_TAU = 0.3989422804014327
+
+
+def group_indices(local, mesh_ax):
+    front = lax.all_gather(local, mesh_ax)
+    return jnp.sum(front, axis=0)
 
 
 def layer_norm(values, scale_in, shift_in):
@@ -312,7 +317,7 @@
         )
         grad, dense, expert_part = layer_backward(grad, saved)
         totals = (
-            lax.psum(dense[0].astype(jnp.bfloat16), "expert").astype(jnp.float32),
+            group_indices(dense[0].astype(jnp.bfloat16), "expert").astype(jnp.float32),
             lax.psum(dense[1].astype(jnp.bfloat16), "expert").astype(jnp.float32),
             lax.psum(dense[2].astype(jnp.bfloat16), "expert").astype(jnp.float32),
             lax.psum(dense[3].astype(jnp.bfloat16), "expert").astype(jnp.float32),

time: 1100 us -> 1240 us (1.13)
  waiting for transfers between devices: 495 us -> 623 us
    all_gather x0 -> x2, waiting for transfers between devices: none -> 100 us  [group_indices(): front = lax.all_gather(local, mesh_ax)]
    unnamed x27 -> x29, waiting for transfers between devices: 147 us -> 179 us
  transfers between devices with their start and end apart: 27 -> 29, of which waited for: 16 -> 19; matrix products, arithmetic and copies ran while one was open for 23% -> 21% of each run, Pallas kernels for 0% -> 0%
where the time goes in v1:
time: 1240 us; the launch traced here: 1230 us
  waiting for transfers between devices  623 us (50%)
  local copies, waits for them, and re-layouts  187 us (15%)
  blocking collectives  182 us (15%)
  matrix products  151 us (12%)
  other arithmetic  45.8 us (4%)
  starting transfers between devices  27.4 us (2%)
  between operations  16.3 us (1%)
    unnamed x29, waiting for transfers between devices  179 us
    reduce_scatter x2, waiting for transfers between devices, body(): lax.psum_scatter(expert_part[1].astype(jnp.bfloat16), 'dp', scatter_dimen...  101 us
    all_gather x2, waiting for transfers between devices, group_indices(): front = lax.all_gather(local, mesh_ax)  100 us
    reduce_scatter x2, waiting for transfers between devices, body(): lax.psum_scatter(expert_part[0].astype(jnp.bfloat16), 'dp', scatter_dimen...  98.6 us
    reduce_scatter x2, waiting for transfers between devices, body(): lax.psum_scatter(totals[0].astype(jnp.bfloat16), 'dp', scatter_dimension=...  67.2 us
    all_gather x2, blocking collectives, layer_forward(): lax.all_gather(w_proj[which], 'dp', axis=0, tiled=True)  40.2 us
    all_to_all x2, blocking collectives, layer_backward(): lax.all_to_all(slot_grads, 'expert', split_axis=0, concat_axis=0, tiled=T...  36.8 us
    all_gather x2, blocking collectives, layer_forward(): lax.all_gather(w_router[which], 'dp', axis=0, tiled=True)  32.6 us
  transfers between devices with their start and end apart: 29, of which 19 were waited for; matrix products, arithmetic and copies ran while one was open for 21% of the time, Pallas kernels for 0%

profile of v1, /device:TPU:0, one launch (start us, length us, event | category | flops | bytes accessed | tf_op | source)
XLA Modules:
  0.0 1232.4 jit_solution(3108778533894409035)
XLA Ops:
  16.5 17.0 %all-gather = bf16[1,2,512]{1,0,2:T(2,128)(2,1)S(1)} all-gather(bf16[1,2,64]{1,0,2:T(2,128)(2,1)S(1)} %copy.377), channel_id=2, replica_groups=mesh['dp'=8,'expert'=4] {'dp'}, dimensions={2}, use_global_device_ids=true | all-gather | bytes 2304 | tf_op jit(solution)/shard_map/all_gather | solution.py:61
  55.9 20.8 %all-gather.3 = bf16[1,512,512]{2,1,0:T(8,128)(2,1)} all-gather(bf16[1,64,512]{2,1,0:T(8,128)(2,1)S(1)} %get-tuple-element.124), channel_id=5, replica_groups=mesh['dp'=8,'expert'=4] {'dp'}, dimensions={1}, use_global_device_ids=true | all-gather | bytes 589824 | tf_op jit(solution)/shard_map/all_gather | solution.py:59
  118.4 17.5 %all-gather.4 = bf16[1,512,8]{2,0,1:T(2,128)(2,1)S(1)} all-gather(bf16[1,64,8]{2,0,1:T(2,128)(2,1)} %copy.379), channel_id=6, replica_groups=mesh['dp'=8,'expert'=4] {'dp'}, dimensions={1}, use_global_device_ids=true | all-gather | bytes 9216 | tf_op jit(solution)/shard_map/all_gather | solution.py:60
  153.6 15.8 %all-gather.8 = bf16[1,2,512]{1,0,2:T(2,128)(2,1)S(1)} all-gather(bf16[1,2,64]{1,0,2:T(2,128)(2,1)} %copy.381), channel_id=10, replica_groups=mesh['dp'=8,'expert'=4] {'dp'}, dimensions={2}, use_global_device_ids=true | all-gather | bytes 2304 | tf_op jit(solution)/shard_map/all_gather | solution.py:62
  204.2 19.4 %all-gather.10 = bf16[1,512,512]{2,1,0:T(8,128)(2,1)} all-gather(bf16[1,64,512]{2,1,0:T(8,128)(2,1)S(1)} %copy-done.50), channel_id=12, replica_groups=mesh['dp'=8,'expert'=4] {'dp'}, dimensions={1}, use_global_device_ids=true | all-gather | bytes 589824 | tf_op jit(solution)/shard_map/all_gather | solution.py:59
  287.2 15.1 %all-gather.11 = bf16[1,512,8]{2,0,1:T(2,128)(2,1)S(1)} all-gather(bf16[1,64,8]{2,0,1:T(2,128)(2,1)} %copy.382), channel_id=13, replica_groups=mesh['dp'=8,'expert'=4] {'dp'}, dimensions={1}, use_global_device_ids=true | all-gather | bytes 9216 | tf_op jit(solution)/shard_map/all_gather | solution.py:60
  330.7 14.8 %all-to-all-done.3 = bf16[4,2,147,512]{3,1,2,0:T(2,128)(2,1)} async-done(((bf16[4,2,147,512]{3,1,2,0:T(2,128)(2,1)}), bf16[4,2,147,512]{3,1,2,0:T(2,128)(2,1)}, u32[]{:S(2)}, u32[]{:S(2)}) %all-to-all-start.3) | async-done | bytes 1204256 | tf_op jit(solution)/shard_map/all_to_all | solution.py:115
  369.8 18.6 %all_to_all.44 = bf16[4,2,147,512]{3,1,2,0:T(2,128)(2,1)S(1)} all-to-all(bf16[4,2,147,512]{3,1,2,0:T(2,128)(2,1)S(1)} %copy.295), channel_id=1, replica_groups=mesh['dp'=8,'expert'=4] {'expert'}, dimensions={0} | all-to-all | bytes 2408448 | tf_op jit(solution)/shard_map/all_to_all | solution.py:205
  470.5 18.2 %all_to_all.45 = bf16[4,2,147,512]{3,1,2,0:T(2,128)(2,1)S(1)} all-to-all(bf16[4,2,147,512]{3,1,2,0:T(2,128)(2,1)S(1)} %copy.311), channel_id=1, replica_groups=mesh['dp'=8,'expert'=4] {'expert'}, dimensions={0} | all-to-all | bytes 2408448 | tf_op jit(solution)/shard_map/all_to_all | solution.py:205
  611.1 34.1 %all-gather.39.cloned.1.call-done = bf16[2048,1536]{1,0:T(8,128)(2,1)} async-done(((bf16[512,1536]{1,0:T(8,128)(2,1)}), bf16[2048,1536]{1,0:T(8,128)(2,1)}) %all-gather.39.cloned.1.call-update) | async-done | bytes 6291472 | tf_op jit(solution)/shard_map/all_gather | solution.py:16
  650.7 66.3 %all-gather.37.cloned.1.call-done = bf16[2048,1536]{1,0:T(8,128)(2,1)} async-done(((bf16[512,1536]{1,0:T(8,128)(2,1)}), bf16[2048,1536]{1,0:T(8,128)(2,1)}) %all-gather.37.cloned.1.call-update) | async-done | bytes 6291472 | tf_op jit(solution)/shard_map/all_gather | solution.py:16
  722.4 28.0 %reduce-scatter.45.cloned.1.call-done = bf16[64,8]{1,0:T(8,128)(2,1)} async-done(((bf16[512,8]{1,0:T(8,128)(2,1)}), bf16[64,8]{1,0:T(8,128)(2,1)}) %reduce-scatter.45.cloned.1.call-update) | async-done | bytes 1040
  752.3 28.9 %reduce-scatter.53.cloned.1.call-done = bf16[64,2]{1,0:T(8,128)(2,1)} async-done(((bf16[512,2]{1,0:T(8,128)(2,1)}), bf16[64,2]{1,0:T(8,128)(2,1)}) %reduce-scatter.53.cloned.1.call-update) | async-done | bytes 272
  782.0 30.8 %reduce-scatter.49.cloned.1.call-done = bf16[64,2]{1,0:T(8,128)(2,1)} async-done(((bf16[512,2]{1,0:T(8,128)(2,1)}), bf16[64,2]{1,0:T(8,128)(2,1)}) %reduce-scatter.49.cloned.1.call-update) | async-done | bytes 272
  813.6 30.6 %reduce-scatter.43.cloned.1.call-done = bf16[64,8]{1,0:T(8,128)(2,1)} async-done(((bf16[512,8]{1,0:T(8,128)(2,1)}), bf16[64,8]{1,0:T(8,128)(2,1)}) %reduce-scatter.43.cloned.1.call-update) | async-done | bytes 1040
  847.0 28.1 %reduce-scatter.51.cloned.1.call-done = bf16[64,2]{1,0:T(8,128)(2,1)} async-done(((bf16[512,2]{1,0:T(8,128)(2,1)}), bf16[64,2]{1,0:T(8,128)(2,1)}) %reduce-scatter.51.cloned.1.call-update) | async-done | bytes 272
  875.8 30.7 %reduce-scatter.47.cloned.1.call-done = bf16[64,2]{1,0:T(8,128)(2,1)} async-done(((bf16[512,2]{1,0:T(8,128)(2,1)}), bf16[64,2]{1,0:T(8,128)(2,1)}) %reduce-scatter.47.cloned.1.call-update) | async-done | bytes 272
  919.1 30.6 %all-reduce.6.cloned.1.call-done = (bf16[64,512]{1,0:T(8,128)(2,1)}, bf16[64,512]{1,0:T(8,128)(2,1)}) async-done(((bf16[64,512]{1,0:T(8,128)(2,1)}, bf16[64,512]{1,0:T(8,128)(2,1)}), (bf16[64,512]{1,0:T(8,128)(2,1)}, bf16[64,512]{1,0:T(8,128)(2,1)})) %all-reduce.6.cloned.1.call-update) | async-done | bytes 131088 | tf_op jit(solution)/shard_map/psum | solution.py:321
  951.3 50.5 %reduce-scatter.37.cloned.1.call-done = bf16[2,256,512]{2,1,0:T(8,128)(2,1)} async-done(((bf16[2,2048,512]{2,1,0:T(8,128)(2,1)}), bf16[2,256,512]{2,1,0:T(8,128)(2,1)}) %reduce-scatter.37.cloned.1.call-update) | async-done | bytes 524304 | tf_op jit(solution)/shard_map/reduce_scatter | solution.py:347
  1001.8 50.7 %reduce-scatter.35.cloned.1.call-done = bf16[2,256,512]{2,1,0:T(8,128)(2,1)} async-done(((bf16[2,2048,512]{2,1,0:T(8,128)(2,1)}), bf16[2,256,512]{2,1,0:T(8,128)(2,1)}) %reduce-scatter.35.cloned.1.call-update) | async-done | bytes 524304 | tf_op jit(solution)/shard_map/reduce_scatter | solution.py:347
  1055.2 47.9 %reduce-scatter.33.cloned.1.call-done = bf16[2,512,256]{2,1,0:T(8,128)(2,1)} async-done(((bf16[2,512,2048]{2,1,0:T(8,128)(2,1)}), bf16[2,512,256]{2,1,0:T(8,128)(2,1)}) %reduce-scatter.33.cloned.1.call-update) | async-done | bytes 524304 | tf_op jit(solution)/shard_map/reduce_scatter | solution.py:344
  1103.1 50.7 %reduce-scatter.31.cloned.1.call-done = bf16[2,512,256]{2,1,0:T(8,128)(2,1)} async-done(((bf16[2,512,2048]{2,1,0:T(8,128)(2,1)}), bf16[2,512,256]{2,1,0:T(8,128)(2,1)}) %reduce-scatter.31.cloned.1.call-update) | async-done | bytes 524304 | tf_op jit(solution)/shard_map/reduce_scatter | solution.py:344
  1156.5 32.3 %reduce-scatter.29.cloned.1.call-done = bf16[64,1536]{1,0:T(8,128)(2,1)} async-done(((bf16[512,1536]{1,0:T(8,128)(2,1)}), bf16[64,1536]{1,0:T(8,128)(2,1)}) %reduce-scatter.29.cloned.1.call-update) | async-done | bytes 196624 | tf_op jit(solution)/shard_map/reduce_scatter | solution.py:327
  1188.8 34.9 %reduce-scatter.27.cloned.1.call-done = bf16[64,1536]{1,0:T(8,128)(2,1)} async-done(((bf16[512,1536]{1,0:T(8,128)(2,1)}), bf16[64,1536]{1,0:T(8,128)(2,1)}) %reduce-scatter.27.cloned.1.call-update) | async-done | bytes 196624 | tf_op jit(solution)/shard_map/reduce_scatter | solution.py:327
  (603 shorter events, 483.7 us)
Async XLA Ops:
  7.2 76.4 %all-gather.25.cloned.1.call-start = ((), (), s32[]{:S(2)}) async-start(), calls=%async_computation.28 | async-start | bytes 1769472 | tf_op jit(solution)/shard_map/all_gather | solution.py:58
  9.1 172.3 %all-gather.27.cloned.1.call-start = ((), (), s32[]{:S(2)}) async-start(), calls=%async_computation.29 | async-start | bytes 4718592 | tf_op jit(solution)/shard_map/all_gather | solution.py:65
  11.5 179.1 %all-gather.29.cloned.1.call-start = ((), (), s32[]{:S(2)}) async-start(), calls=%async_computation.30 | async-start | bytes 4718592 | tf_op jit(solution)/shard_map/all_gather | solution.py:66
  12.6 229.4 %all-gather.31.cloned.1.call-start = ((), (), s32[]{:S(2)}) async-start(), calls=%async_computation.31 | async-start | bytes 1769472 | tf_op jit(solution)/shard_map/all_gather | solution.py:58
  13.2 294.0 %all-gather.33.cloned.1.call-start = ((), (), s32[]{:S(2)}) async-start(), calls=%async_computation.32 | async-start | bytes 4718592 | tf_op jit(solution)/shard_map/all_gather | solution.py:65
  13.8 302.5 %all-gather.35.cloned.1.call-start = ((), (), s32[]{:S(2)}) async-start(), calls=%async_computation.33 | async-start | bytes 4718592 | tf_op jit(solution)/shard_map/all_gather | solution.py:66
  114.1 67.3 %all-to-all-start = ((bf16[4,2,147,512]{3,1,2,0:T(2,128)(2,1)}), bf16[4,2,147,512]{3,1,2,0:T(2,128)(2,1)}, u32[]{:S(2)}, u32[]{:S(2)}) async-start(bf16[4,2,147,512]{3,1,2,0:T(2,128)(2,1)} %copy.273), calls=%async_computation | async-start | bytes 2408448 | tf_op jit(solution)/shard_map/all_to_all | solution.py:107
  506.3 62.2 %reduce-scatter.41.cloned.1.call-start = ((), (), s32[]{:S(2)}) async-start(), calls=%async_computation.37 | async-start | bytes 589824 | tf_op jit(solution)/shard_map/reduce_scatter | solution.py:330
  508.9 65.8 %reduce-scatter.39.cloned.1.call-start = ((), (), s32[]{:S(2)}) async-start(), calls=%async_computation.36 | async-start | bytes 589824 | tf_op jit(solution)/shard_map/reduce_scatter | solution.py:330
  531.2 114.0 %all-gather.39.cloned.1.call-start = ((), (), s32[]{:S(2)}) async-start(), calls=%async_computation.35 | async-start | bytes 7864320 | tf_op jit(solution)/shard_map/all_gather | solution.py:16
  535.3 181.6 %all-gather.37.cloned.1.call-start = ((), (), s32[]{:S(2)}) async-start(), calls=%async_computation.34 | async-start | bytes 7864320 | tf_op jit(solution)/shard_map/all_gather | solution.py:16
  559.2 191.2 %reduce-scatter.45.cloned.1.call-start = ((), (), s32[]{:S(2)}) async-start(), calls=%async_computation.39 | async-start | bytes 147456
  560.2 221.0 %reduce-scatter.53.cloned.1.call-start = ((), (), s32[]{:S(2)}) async-start(), calls=%async_computation.43 | async-start | bytes 147456
  561.2 251.6 %reduce-scatter.49.cloned.1.call-start = ((), (), s32[]{:S(2)}) async-start(), calls=%async_computation.41 | async-start | bytes 147456
  562.1 282.1 %reduce-scatter.43.cloned.1.call-start = ((), (), s32[]{:S(2)}) async-start(), calls=%async_computation.38 | async-start | bytes 147456
  563.1 311.9 %reduce-scatter.51.cloned.1.call-start = ((), (), s32[]{:S(2)}) async-start(), calls=%async_computation.42 | async-start | bytes 147456
  567.5 339.0 %reduce-scatter.47.cloned.1.call-start = ((), (), s32[]{:S(2)}) async-start(), calls=%async_computation.40 | async-start | bytes 147456
  568.4 381.3 %all-reduce.6.cloned.1.call-start = ((), (), s32[]{:S(2)}) async-start(), calls=%async_computation.44 | async-start | bytes 262144 | tf_op jit(solution)/shard_map/psum | solution.py:321
  574.7 427.1 %reduce-scatter.37.cloned.1.call-start = ((), (), s32[]{:S(2)}) async-start(), calls=%async_computation.27 | async-start | bytes 4718592 | tf_op jit(solution)/shard_map/reduce_scatter | solution.py:347
  583.7 468.8 %reduce-scatter.35.cloned.1.call-start = ((), (), s32[]{:S(2)}) async-start(), calls=%async_computation.26 | async-start | bytes 4718592 | tf_op jit(solution)/shard_map/reduce_scatter | solution.py:347
  593.8 509.3 %reduce-scatter.33.cloned.1.call-start = ((), (), s32[]{:S(2)}) async-start(), calls=%async_computation.25 | async-start | bytes 4718592 | tf_op jit(solution)/shard_map/reduce_scatter | solution.py:344
  602.2 551.6 %reduce-scatter.31.cloned.1.call-start = ((), (), s32[]{:S(2)}) async-start(), calls=%async_computation.24 | async-start | bytes 4718592 | tf_op jit(solution)/shard_map/reduce_scatter | solution.py:344
  611.0 577.8 %reduce-scatter.29.cloned.1.call-start = ((), (), s32[]{:S(2)}) async-start(), calls=%async_computation.23 | async-start | bytes 1769472 | tf_op jit(solution)/shard_map/reduce_scatter | solution.py:327
  650.7 573.0 %reduce-scatter.27.cloned.1.call-start = ((), (), s32[]{:S(2)}) async-start(), calls=%async_computation.22 | async-start | bytes 1769472 | tf_op jit(solution)/shard_map/reduce_scatter | solution.py:327
  (144 other events, 1640.9 us)
Sparse Core Ops, SparseCore 0:
  10.2 29.4 all-gather.24
  41.3 51.4 all-gather.26
  94.4 47.3 all-gather.28
  143.9 25.6 all-gather.30
  171.0 50.4 all-gather.32
  222.9 45.9 all-gather.34
  509.3 33.6 reduce-scatter.40
  545.3 29.3 reduce-scatter.38
  577.1 68.0 all-gather.38
  646.9 70.0 all-gather.36
  719.8 30.5 reduce-scatter.44
  752.5 28.7 reduce-scatter.52
  784.1 28.7 reduce-scatter.48
  815.5 28.7 reduce-scatter.42
  846.3 28.6 reduce-scatter.50
  877.7 28.7 reduce-scatter.46
  909.2 40.4 all-reduce.5
  951.9 49.8 reduce-scatter.36
  1004.1 48.3 reduce-scatter.34
  1054.7 48.3 reduce-scatter.32
  1105.4 48.3 reduce-scatter.30
  1156.1 32.6 reduce-scatter.28
  1191.1 32.5 reduce-scatter.26
